TPU v7x, 256 devices: a whole 4x4x8 slice. The times are simulated.
256 devices in a mesh: space: 32 (over z, x), tm: 8 (over y, core).
Axes of the slice: x: 4, y: 4, z: 8, core: 2. Of those that a mesh axis runs over, the one named last changes fastest.
Arguments:
- iterate: float32 [8, 240, 23040], P(None, 'tm', 'space'), may hold values from -6 to 6
- residual: float32 [8, 240, 23040], P(None, 'tm', 'space'), may hold values from -24 to 24
- direction: float32 [8, 240, 23040], P(None, 'tm', 'space'), may hold values from -24 to 24
- diffusivity: float32 [23040], P('space'), may hold values from 0.1 to 0.34
- temporal_factor: float32 [240, 240], replicated, may hold values from 0 to 4
- block_tile: int32 [8, 256], P('tm', 'space'), may hold values from -1 to 479, as said below
- footprints: bfloat16 [8, 256, 64, 1440], P('tm', 'space'), may hold values from -0.15625 to 0.15625
- obs_weight: float32 [8, 32, 64], P('tm', 'space'), may hold values from 0.3 to 3
Outputs:
- iterate_next: float32 [8, 240, 23040], P(None, 'tm', 'space')
- residual_next: float32 [8, 240, 23040], P(None, 'tm', 'space')
- direction_next: float32 [8, 240, 23040], P(None, 'tm', 'space')
Inputs may be any that keep to these rules, and one draw needn't show every extreme that they name: `block_tile`: entry -1 marks a padding slot. Tile g belongs to index g // 15 of space. The valid entries of one device name distinct tiles, at most 2 of them of one owner; in each row of tm one owner is named exactly 2 times by every device.
All inputs are finite; a program needn't handle non-finite values.
Results may differ from a plain program's by a relative error of at most 0.017.
Values may be sent and summed in bfloat16 or wider, within the bound.
No kernel may reach another device: no remote copies, remote signals or barrier semaphores. Data moves between devices by JAX's collectives and lax.ppermute only.
A program may use at most 128 MiB of HBM per device.

v0:
```python
import jax
import jax.numpy as jnp
from jax import lax
from jax.sharding import PartitionSpec as P

LON = 720
TC = 48
NB = 8
DIFF = 2


def for_sending(value):

    def short(part):
        return part.astype(jnp.bfloat16) if part.dtype == jnp.float32 else part

    return jax.tree.map(short, value)


def extended_2(cells, sides, width):
    for axis, dim in sides:
        count = lax.axis_size(axis)
        ends = count - 1
        head = lax.slice_in_dim(cells, 0, width, axis=dim)
        tail = lax.slice_in_dim(cells, cells.shape[dim] - width, cells.shape[dim], axis=dim)
        cells = jnp.concatenate(
            [
                lax.ppermute(tail, axis, [(i, (i + 1) % count) for i in range(ends)]),
                cells,
                lax.ppermute(head, axis, [((i + 1) % count, i) for i in range(ends)]),
            ],
            axis=dim,
        )
    return cells


def temporal(field, matrix):
    combined = jnp.einsum(
        "tu,kuc->ktc",
        matrix,
        lax.all_to_all(
            field.astype(jnp.bfloat16), "tm", split_axis=2, concat_axis=1, tiled=True
        ).astype(field.dtype),
        precision=lax.Precision.HIGHEST,
    )
    return lax.all_to_all(
        for_sending(combined), "tm", split_axis=1, concat_axis=2, tiled=True
    ).astype(combined.dtype)


def diffuse(field, conduct):
    samples, window, cell_count = field.shape
    rows_here = cell_count // LON
    for sweep_index in range(DIFF):
        scaled_field = field * conduct
        extended = extended_2(for_sending(scaled_field), (("space", 2),), LON).astype(
            scaled_field.dtype
        )
        planes = extended.reshape(samples, window, rows_here + 2, LON)
        centre = planes[:, :, 1:-1, :]
        laplace = (
            planes[:, :, :-2, :]
            + planes[:, :, 2:, :]
            + jnp.roll(centre, 1, 3)
            + jnp.roll(centre, -1, 3)
            - 4.0 * centre
        )
        field = field + conduct * laplace.reshape(samples, window, cell_count)
    return field


def local(
    iterate, residual, direction, diffusivity, temporal_factor, block_tile, footprints, obs_weight
):
    samples, window, cell_count = direction.shape
    tiles_here = cell_count // TC
    entries = block_tile[0]
    blocks_here = entries.shape[0]
    present = entries >= 0
    mixed = temporal(direction, temporal_factor)
    spread = diffuse(mixed, diffusivity)
    tiled = spread.astype(jnp.bfloat16).reshape(samples, window, tiles_here, TC)
    empty_blocks = jnp.zeros((blocks_here, samples, window * TC), jnp.float32)
    segment = lax.all_gather(tiled, "space", axis=2, tiled=True)
    count_tiles = segment.shape[2]
    selector = (entries[:, None] == jnp.arange(count_tiles)[None, :]).astype(jnp.bfloat16)
    picked = jnp.einsum("bj,ktjc->bktc", selector, segment, preferred_element_type=jnp.float32)
    blocks = picked.reshape(empty_blocks.shape).astype(jnp.bfloat16)
    footprint = footprints[0]
    batches = obs_weight.shape[1]
    slot_obs = jnp.einsum("bmx,bkx->bkm", footprint, blocks, preferred_element_type=jnp.float32)
    batch_obs = jnp.sum(slot_obs.reshape(batches, NB, samples, footprint.shape[1]), axis=1)
    weighted = (obs_weight[0][:, None, :] * batch_obs).astype(jnp.bfloat16)
    grouped = footprint.reshape(batches, NB, footprint.shape[1], footprint.shape[2])
    gradient = jnp.einsum("anmx,akm->ankx", grouped, weighted, preferred_element_type=jnp.float32)
    gradient = gradient.reshape(blocks_here, samples, footprint.shape[2])
    gradient = jnp.where(present[:, None, None], gradient, 0.0).astype(jnp.bfloat16)
    selector = (
        entries[:, None] == jnp.arange(lax.axis_size("space") * tiles_here)[None, :]
    ).astype(jnp.bfloat16)
    summed = lax.psum_scatter(
        jnp.einsum("bj,bkx->jkx", selector, gradient, preferred_element_type=jnp.float32).astype(
            jnp.bfloat16
        ),
        "space",
        scatter_dimension=0,
        tiled=True,
    ).astype(jnp.float32)
    pulled = (
        summed.reshape(tiles_here, samples, window, TC)
        .transpose(1, 2, 0, 3)
        .reshape(samples, window, cell_count)
    )
    back = diffuse(pulled, diffusivity)
    image = direction + temporal(back, temporal_factor.T)
    old_norm, curvature = lax.psum(
        (jnp.sum(residual * residual, axis=(1, 2)), jnp.sum(direction * image, axis=(1, 2))),
        ("space", "tm"),
    )
    step_size = old_norm / curvature
    residual_next = residual - step_size[:, None, None] * image
    new_norm = lax.psum(jnp.sum(residual_next * residual_next, axis=(1, 2)), ("space", "tm"))
    iterate_next = iterate + step_size[:, None, None] * direction
    direction_next = residual_next + (new_norm / old_norm)[:, None, None] * direction
    return (iterate_next, residual_next, direction_next)


def solution(mesh):
    return jax.shard_map(
        local,
        mesh=mesh,
        in_specs=(
            P(None, "tm", "space"),
            P(None, "tm", "space"),
            P(None, "tm", "space"),
            P("space"),
            P(),
            P("tm", "space"),
            P("tm", "space", None, None),
            P("tm", "space", None),
        ),
        out_specs=(P(None, "tm", "space"), P(None, "tm", "space"), P(None, "tm", "space")),
        check_vma=False,
    )
```

profile of v0, /device:TPU:1, one launch (start us, length us, event | category | flops | bytes accessed | tf_op | source)
XLA Modules:
  0.0 833.4 jit_solution(11026537258770947451)
XLA Ops:
  7.2 1.3 convert_element_type.141
  8.5 1.5 copy.95
  10.0 2.0 reshape.151
  12.0 14.0 %all_to_all.54 = bf16[8,2,10800]{2,1,0:T(2,128)(2,1)} all-to-all(bf16[8,2,10800]{2,1,0:T(2,128)(2,1)S(1)} %reshape.151), channel_id=1, replica_groups=mesh['space'=32,'tm'=8] {'tm'}, dimensions={0} | all-to-all | bytes 691200 | tf_op jit(solution)/shard_map/all_to_all | solution.py:41
  26.0 3.1 reshape.152
  30.2 1.6 fusion.12
  32.1 12.3 %all_to_all.55 = bf16[8,240,90]{2,0,1:T(8,128)(2,1)S(1)} all-to-all(bf16[8,240,90]{2,0,1:T(8,128)(2,1)S(1)} %copy.98), channel_id=1, replica_groups=mesh['space'=32,'tm'=8] {'tm'}, dimensions={1} | all-to-all | bytes 691200 | tf_op jit(solution)/shard_map/all_to_all | solution.py:46
  46.0 1.9 multiply_convert_fusion.6
  47.9 3.4 collective-permute-start
  51.3 1.3 collective-permute-start.1
  54.9 2.8 collective-permute-done
  57.7 4.6 collective-permute-done.1
  62.3 1.3 maximum_convert_fusion
  67.5 3.1 collective-permute-start.2
  70.7 1.5 collective-permute-start.3
  72.2 1.3 copy.99
  73.5 2.7 reshape.137
  76.2 3.1 reshape.128
  81.4 1.4 maximum_convert_fusion.1
  83.1 1.2 fusion.38
  84.3 3.1 reshape.130
  87.4 4.9 fusion.5
  93.8 215.8 %all-gather.2.cloned.1.call-done = bf16[8,30,480,48]{3,0,1,2:T(8,128)(2,1)} async-done(((bf16[8,30,15,48]{3,0,1,2:T(8,128)(2,1)}), bf16[8,30,480,48]{3,0,1,2:T(8,128)(2,1)}) %all-gather.2.cloned.1.call-update) | async-done | bytes 11059216 | tf_op jit(solution)/shard_map/all_gather | solution.py:84
  309.6 26.4 %fusion.9 = bf16[8,8,30,48]{3,0,2,1:T(8,128)(2,1)S(1)} fusion(bf16[8,30,480,48]{3,0,1,2:T(8,128)(2,1)} %all-gather.2.cloned.1.call-done, s32[8]{0:T(128)S(1)} %bitcast.153), kind=kOutput, calls=%fused_computation.14 | convolution fusion | flops 88569600 | bytes 11243552 | tf_op jit(solution)/shard_map/bj,ktjc->bktc/dot_general | solution.py:87
  336.9 1.2 fusion.3
  338.1 3.7 convolution_convert_fusion
  341.8 20.4 %copy.109 = bf16[480,8,1440]{2,1,0:T(8,128)(2,1)} copy(bf16[480,8,1440]{2,0,1:T(8,128)(2,1)S(1)} %convolution_convert_fusion) | data formatting | bytes 22118400 | tf_op jit(solution)/shard_map/convert_element_type | solution.py:102
  362.2 230.0 %reduce-scatter.2.cloned.1.call-done = bf16[15,8,1440]{2,1,0:T(8,128)(2,1)} async-done(((bf16[480,8,1440]{2,1,0:T(8,128)(2,1)}), bf16[15,8,1440]{2,1,0:T(8,128)(2,1)}) %reduce-scatter.2.cloned.1.call-update) | async-done | bytes 345616 | tf_op jit(solution)/shard_map/reduce_scatter | solution.py:101
  592.2 3.0 reshape.141
  595.3 2.6 copy.110
  599.5 3.0 collective-permute-start.4
  602.5 1.3 collective-permute-start.5
  604.7 1.8 collective-permute-done.4
  606.5 4.6 collective-permute-done.5
  611.1 1.3 maximum_convert_fusion.2
  614.2 2.7 collective-permute-start.6
  616.9 1.5 collective-permute-start.7
  618.4 2.9 collective-permute-done.6
  621.4 3.8 collective-permute-done.7
  626.3 1.5 copy.112
  627.8 2.0 reshape.153
  629.8 19.2 %all_to_all.56 = bf16[8,2,10800]{2,1,0:T(2,128)(2,1)S(1)} all-to-all(bf16[8,2,10800]{2,1,0:T(2,128)(2,1)S(1)} %reshape.153), channel_id=1, replica_groups=mesh['space'=32,'tm'=8] {'tm'}, dimensions={0} | all-to-all | bytes 691200 | tf_op jit(solution)/shard_map/all_to_all | solution.py:41
  649.0 1.8 reshape.154
  652.8 12.3 %all_to_all.57 = bf16[8,240,90]{2,0,1:T(8,128)(2,1)S(1)} all-to-all(bf16[8,240,90]{2,0,1:T(8,128)(2,1)S(1)} %copy.116), channel_id=1, replica_groups=mesh['space'=32,'tm'=8] {'tm'}, dimensions={1} | all-to-all | bytes 691200 | tf_op jit(solution)/shard_map/all_to_all | solution.py:46
  667.8 81.2 %all-reduce = (f32[8]{0:T(128)S(1)}, f32[8]{0:T(128)S(1)}) all-reduce(f32[8]{0:T(128)S(1)} %get-tuple-element.31, f32[8]{0:T(128)S(1)} %get-tuple-element.7), channel_id=1, replica_groups=mesh['space'=32,'tm'=8] {'space','tm'}, use_global_device_ids=true, to_apply=%region_1.2 | all-reduce | flops 16 | bytes 128 | tf_op jit(solution)/shard_map/psum | solution.py:116
  749.0 1.5 multiply_reduce_fusion
  750.5 73.2 %psum.23 = f32[8]{0:T(128)S(1)} all-reduce(f32[8]{0:T(128)S(1)} %get-tuple-element.5), channel_id=1, replica_groups=mesh['space'=32,'tm'=8] {'space','tm'}, use_global_device_ids=true, to_apply=%region_6.7 | all-reduce | flops 8 | bytes 64 | tf_op jit(solution)/shard_map/psum | solution.py:122
  823.8 2.5 multiply_add_fusion
  (73 shorter events, 24.1 us)
Async XLA Ops:
  7.2 329.7 %copy-start = (bf16[1,8,64,1440]{3,2,1,0:T(8,128)(2,1)S(1)}, bf16[1,8,64,1440]{3,2,1,0:T(8,128)(2,1)}, u32[]{:S(2)}) copy-start(bf16[1,8,64,1440]{3,2,1,0:T(8,128)(2,1)} %param.14) | copy-start | bytes 4423684
  7.2 302.4 %all-gather.2.cloned.1.call-start = ((), (), s32[]{:S(2)}) async-start(), calls=%async_computation.5 | async-start | bytes 30412800 | tf_op jit(solution)/shard_map/all_gather | solution.py:84
  44.4 1.5 copy-start.11
  47.9 9.9 %collective-permute-start = (bf16[8,30,720]{2,0,1:T(8,128)(2,1)}, bf16[8,30,720]{2,0,1:T(8,128)(2,1)}, u32[]{:S(2)}, u32[]{:S(2)}) collective-permute-start(bf16[8,30,720]{2,0,1:T(8,128)(2,1)} %multiply_convert_fusion.6), channel_id=1, source_target_pairs={{0,8},{8,16},{16,24},{24,32},{32,40},{40,48},{48,56},{56,64},{64,7... | collective-permute-start | bytes 1036808 | tf_op jit(solution)/shard_map/ppermute | solution.py:28
  51.3 11.0 %collective-permute-start.1 = (bf16[8,30,720]{2,0,1:T(8,128)(2,1)}, bf16[8,30,720]{2,0,1:T(8,128)(2,1)}, u32[]{:S(2)}, u32[]{:S(2)}) collective-permute-start(bf16[8,30,720]{2,0,1:T(8,128)(2,1)} %multiply_convert_fusion.6), channel_id=1, source_target_pairs={{8,0},{16,8},{24,16},{32,24},{40,32},{48,40},{56,48},{64,56},{72,6... | collective-permute-start | bytes 1036808 | tf_op jit(solution)/shard_map/ppermute | solution.py:30
  63.6 1.1 copy-start.3
  64.7 2.0 copy-start.6
  65.8 0.9 copy-start.2
  67.5 11.8 %collective-permute-start.2 = (bf16[8,30,720]{2,0,1:T(8,128)(2,1)}, bf16[8,30,720]{2,0,1:T(8,128)(2,1)}, u32[]{:S(2)}, u32[]{:S(2)}) collective-permute-start(bf16[8,30,720]{2,0,1:T(8,128)(2,1)} %fusion.47), channel_id=1, source_target_pairs={{0,8},{8,16},{16,24},{24,32},{32,40},{40,48},{48,56},{56,64},{64,7... | collective-permute-start | bytes 1036808 | tf_op jit(solution)/shard_map/ppermute | solution.py:28
  70.7 9.8 %collective-permute-start.3 = (bf16[8,30,720]{2,0,1:T(8,128)(2,1)}, bf16[8,30,720]{2,0,1:T(8,128)(2,1)}, u32[]{:S(2)}, u32[]{:S(2)}) collective-permute-start(bf16[8,30,720]{2,0,1:T(8,128)(2,1)} %fusion.47), channel_id=1, source_target_pairs={{8,0},{16,8},{24,16},{32,24},{40,32},{48,40},{56,48},{64,56},{72,6... | collective-permute-start | bytes 1036808 | tf_op jit(solution)/shard_map/ppermute | solution.py:30
  92.3 1.4 copy-start.12
  93.5 498.7 %reduce-scatter.2.cloned.1.call-start = ((), (), s32[]{:S(2)}) async-start(), calls=%async_computation.6 | async-start | bytes 12165120 | tf_op jit(solution)/shard_map/reduce_scatter | solution.py:101
  309.6 27.3 %copy-start.13 = (f32[1,1,64]{2,1,0:T(1,128)S(1)}, f32[1,1,64]{2,1,0:T(1,128)}, u32[]{:S(2)}) copy-start(f32[1,1,64]{2,1,0:T(1,128)} %param.15) | copy-start | bytes 772
  599.5 7.0 collective-permute-start.4
  602.5 8.6 %collective-permute-start.5 = (bf16[8,30,720]{2,0,1:T(8,128)(2,1)}, bf16[8,30,720]{2,0,1:T(8,128)(2,1)}, u32[]{:S(2)}, u32[]{:S(2)}) collective-permute-start(bf16[8,30,720]{2,0,1:T(8,128)(2,1)} %multiply_convert_fusion.3), channel_id=1, source_target_pairs={{8,0},{16,8},{24,16},{32,24},{40,32},{48,40},{56,48},{64,56},{72,6... | collective-permute-start | bytes 1036808 | tf_op jit(solution)/shard_map/ppermute | solution.py:30
  604.7 7.7 copy-start.4
  612.5 1.1 copy-start.5
  614.2 7.1 collective-permute-start.6
  616.9 8.3 collective-permute-start.7
  649.0 2.9 copy-start.10
  665.1 1.1 copy-start.7
  665.5 1.2 copy-start.8
  750.5 75.8 %copy-start.9 = (f32[8,30,720]{2,0,1:T(8,128)}, f32[8,30,720]{2,0,1:T(8,128)S(1)}, u32[]{:S(2)}) copy-start(f32[8,30,720]{2,0,1:T(8,128)S(1)} %get-tuple-element.6) | copy-start | bytes 2073604
  823.8 2.6 copy-start.1
Sparse Core Ops, SparseCore 0:
  93.6 215.9 all-gather.1
  362.4 229.8 reduce-scatter.1
where the time goes:
time: 841 us; the launch traced here: 833 us
  waiting for transfers between devices  468 us (56%)
  blocking collectives  212 us (25%)
  local copies, waits for them, and re-layouts  62.5 us (7%)
  matrix products  33.5 us (4%)
  other arithmetic  25.1 us (3%)
  starting transfers between devices  18 us (2%)
  between operations  14.6 us (2%)
    reduce_scatter x1, waiting for transfers between devices, local(): lax.psum_scatter(jnp.einsum('bj,bkx->jkx', selector, gradient, preferred_...  230 us
    all_gather x1, waiting for transfers between devices, local(): segment = lax.all_gather(tiled, 'space', axis=2, tiled=True)  216 us
    psum x1, blocking collectives, local(): lax.psum((jnp.sum(residual * residual, axis=(1, 2)), jnp.sum(direction *...  81.2 us
    psum x1, blocking collectives, local(): lax.psum(jnp.sum(residual_next * residual_next, axis=(1, 2)), ('space', '...  73.2 us
    all_to_all x2, blocking collectives, temporal(): lax.all_to_all(field.astype(jnp.bfloat16), 'tm', split_axis=2, concat_axi...  33.1 us
    dot_general x1, matrix products, local(): jnp.einsum('bj,ktjc->bktc', selector, segment, preferred_element_type=jnp...  26.4 us
    all_to_all x2, blocking collectives, temporal(): lax.all_to_all(for_sending(combined), 'tm', split_axis=1, concat_axis=2,...  24.5 us
    convert_element_type x1, local copies, waits for them, and re-layouts, local(): jnp.einsum('bj,bkx->jkx', selector, gradient, preferred_element_type=jnp....  20.4 us
  transfers between devices with their start and end apart: 10, of which 9 were waited for; matrix products, arithmetic and copies ran while one was open for 1% of the time, Pallas kernels for 0%

commit v1 on v0

--- a/solution.py
+++ b/solution.py
@@ -81,7 +81,11 @@
     spread = diffuse(mixed, diffusivity)
     tiled = spread.astype(jnp.bfloat16).reshape(samples, window, tiles_here, TC)
     empty_blocks = jnp.zeros((blocks_here, samples, window * TC), jnp.float32)
-    segment = lax.all_gather(tiled, "space", axis=2, tiled=True)
+    size = lax.axis_size("space")
+    repeats = [size if d == 2 else 1 for d in range(tiled.ndim)]
+    segment = lax.all_to_all(
+        jnp.tile(tiled, repeats), "space", split_axis=2, concat_axis=2, tiled=True
+    )
     count_tiles = segment.shape[2]
     selector = (entries[:, None] == jnp.arange(count_tiles)[None, :]).astype(jnp.bfloat16)
     picked = jnp.einsum("bj,ktjc->bktc", selector, segment, preferred_element_type=jnp.float32)

time: 841 us -> 1020 us (1.21)
  local copies, waits for them, and re-layouts: 62.5 us -> 188 us
  waiting for transfers between devices: 468 us -> 499 us
  starting transfers between devices: 18 us -> 32.7 us
    all_to_all x0 -> x1, waiting for transfers between devices: none -> 236 us  [local(): lax.all_to_all(jnp.tile(tiled, repeats), 'space', split_axis=2, concat_ax...]
    all_gather x1 -> x0, waiting for transfers between devices: 216 us -> none  [local(): segment = lax.all_gather(tiled, 'space', axis=2, tiled=True)]
    unnamed x32 -> x28, local copies, waits for them, and re-layouts: 12.3 us -> 106 us
    another operation x0 -> x2, local copies, waits for them, and re-layouts: none -> 30.3 us  [local(): jnp.tile(tiled, repeats)]
    all_to_all x0 -> x1, starting transfers between devices: none -> 15 us  [local(): lax.all_to_all(jnp.tile(tiled, repeats), 'space', split_axis=2, concat_ax...]
    reduce_scatter x1, waiting for transfers between devices: 230 us -> 244 us  [local(): lax.psum_scatter(jnp.einsum('bj,bkx->jkx', selector, gradient, preferred_...]
  transfers between devices with their start and end apart: 10 -> 10, of which waited for: 9 -> 8; matrix products, arithmetic and copies ran while one was open for 1% -> 1% of each run, Pallas kernels for 0% -> 0%
where the time goes in v1:
time: 1020 us; the launch traced here: 1010 us
  waiting for transfers between devices  499 us (49%)
  blocking collectives  212 us (21%)
  local copies, waits for them, and re-layouts  188 us (18%)
  matrix products  34.6 us (3%)
  starting transfers between devices  32.7 us (3%)
  other arithmetic  29.5 us (3%)
  between operations  14.6 us (1%)
    reduce_scatter x1, waiting for transfers between devices, local(): lax.psum_scatter(jnp.einsum('bj,bkx->jkx', selector, gradient, preferred_...  244 us
    all_to_all x1, waiting for transfers between devices, local(): lax.all_to_all(jnp.tile(tiled, repeats), 'space', split_axis=2, concat_ax...  236 us
    unnamed x28, local copies, waits for them, and re-layouts  106 us
    psum x1, blocking collectives, local(): lax.psum((jnp.sum(residual * residual, axis=(1, 2)), jnp.sum(direction *...  81.2 us
    psum x1, blocking collectives, local(): lax.psum(jnp.sum(residual_next * residual_next, axis=(1, 2)), ('space', '...  73.2 us
    all_to_all x2, blocking collectives, temporal(): lax.all_to_all(field.astype(jnp.bfloat16), 'tm', split_axis=2, concat_axi...  33.2 us
    another operation x2, local copies, waits for them, and re-layouts, local(): jnp.tile(tiled, repeats)  30.3 us
    dot_general x1, matrix products, local(): jnp.einsum('bj,ktjc->bktc', selector, segment, preferred_element_type=jnp...  26.6 us
  transfers between devices with their start and end apart: 10, of which 8 were waited for; matrix products, arithmetic and copies ran while one was open for 1% of the time, Pallas kernels for 0%

profile of v1, /device:TPU:1, one launch (start us, length us, event | category | flops | bytes accessed | tf_op | source)
XLA Modules:
  0.0 1010.4 jit_solution(9679598313135398603)
XLA Ops:
  8.5 1.5 copy.97
  10.0 2.0 reshape.172
  12.0 14.0 %all_to_all.59 = bf16[8,2,10800]{2,1,0:T(2,128)(2,1)} all-to-all(bf16[8,2,10800]{2,1,0:T(2,128)(2,1)S(1)} %reshape.172), channel_id=1, replica_groups=mesh['space'=32,'tm'=8] {'tm'}, dimensions={0} | all-to-all | bytes 691200 | tf_op jit(solution)/shard_map/all_to_all | solution.py:41
  25.9 3.1 reshape.173
  30.2 1.6 fusion.12
  32.1 12.3 %all_to_all.60 = bf16[8,240,90]{2,0,1:T(8,128)(2,1)S(1)} all-to-all(bf16[8,240,90]{2,0,1:T(8,128)(2,1)S(1)} %copy.100), channel_id=1, replica_groups=mesh['space'=32,'tm'=8] {'tm'}, dimensions={1} | all-to-all | bytes 691200 | tf_op jit(solution)/shard_map/all_to_all | solution.py:46
  45.9 1.9 multiply_convert_fusion.6
  47.8 3.4 collective-permute-start
  54.8 2.8 collective-permute-done
  57.7 4.6 collective-permute-done.1
  67.5 3.1 collective-permute-start.2
  70.6 1.5 collective-permute-start.3
  73.4 2.7 reshape.158
  76.1 3.1 reshape.149
  84.3 3.1 reshape.151
  87.3 4.9 fusion.5
  92.3 9.9 tile.8
  102.2 20.4 %copy.145 = bf16[8,30,480,48]{3,0,1,2:T(8,128)(2,1)} copy(bf16[8,30,480,48]{3,0,2,1:T(8,128)(2,1)} %bitcast.145) | data formatting | bytes 22118400 | tf_op jit(solution)/shard_map/tile | solution.py:87
  122.5 50.2 %reshape.174 = bf16[32,2,86400]{2,1,0:T(2,128)(2,1)} reshape(bf16[480,30,8,48]{3,2,1,0:T(8,128)(2,1)} %bitcast.146) | data formatting | bytes 22118400
  172.8 15.0 %all-to-all-start.2 = ((bf16[32,2,86400]{2,1,0:T(2,128)(2,1)}), bf16[32,2,86400]{2,1,0:T(2,128)(2,1)}, u32[]{:S(2)}, u32[]{:S(2)}) async-start(bf16[32,2,86400]{2,1,0:T(2,128)(2,1)} %reshape.174), calls=%async_computation.2 | async-start | bytes 22118400 | tf_op jit(solution)/shard_map/all_to_all | solution.py:86
  187.9 235.7 %all-to-all-done.2 = bf16[32,2,86400]{2,1,0:T(2,128)(2,1)} async-done(((bf16[32,2,86400]{2,1,0:T(2,128)(2,1)}), bf16[32,2,86400]{2,1,0:T(2,128)(2,1)}, u32[]{:S(2)}, u32[]{:S(2)}) %all-to-all-start.2) | async-done | bytes 11059232 | tf_op jit(solution)/shard_map/all_to_all | solution.py:86
  423.5 42.2 %reshape.175 = bf16[480,30,8,48]{3,2,1,0:T(8,128)(2,1)} reshape(bf16[32,2,86400]{2,1,0:T(2,128)(2,1)} %all-to-all-done.2) | data formatting | bytes 22118400
  465.7 26.6 %fusion.9 = bf16[8,8,30,48]{3,0,2,1:T(8,128)(2,1)S(1)} fusion(bf16[8,30,480,48]{3,0,1,2:T(8,128)(2,1)} %bitcast.147, s32[8]{0:T(128)S(1)} %bitcast.161), kind=kOutput, calls=%fused_computation.14 | convolution fusion | flops 88569600 | bytes 11243552 | tf_op jit(solution)/shard_map/bj,ktjc->bktc/dot_general | solution.py:91
  494.4 3.7 convolution_convert_fusion
  498.1 20.4 %copy.111 = bf16[480,8,1440]{2,1,0:T(8,128)(2,1)} copy(bf16[480,8,1440]{2,0,1:T(8,128)(2,1)S(1)} %convolution_convert_fusion) | data formatting | bytes 22118400 | tf_op jit(solution)/shard_map/convert_element_type | solution.py:106
  518.5 243.8 %reduce-scatter.2.cloned.1.call-done = bf16[15,8,1440]{2,1,0:T(8,128)(2,1)} async-done(((bf16[480,8,1440]{2,1,0:T(8,128)(2,1)}), bf16[15,8,1440]{2,1,0:T(8,128)(2,1)}) %reduce-scatter.2.cloned.1.call-update) | async-done | bytes 345616 | tf_op jit(solution)/shard_map/reduce_scatter | solution.py:105
  762.4 3.0 reshape.162
  765.4 2.6 copy.112
  768.1 1.7 reshape.154
  769.7 1.9 multiply_convert_fusion.3
  771.6 3.0 collective-permute-start.4
  775.9 1.7 reshape.155
  778.8 4.4 collective-permute-done.5
  786.8 2.6 collective-permute-start.6
  789.5 1.5 collective-permute-start.7
  790.9 2.9 collective-permute-done.6
  793.9 3.8 collective-permute-done.7
  798.7 1.5 copy.114
  800.3 2.0 reshape.176
  802.2 19.2 %all_to_all.61 = bf16[8,2,10800]{2,1,0:T(2,128)(2,1)} all-to-all(bf16[8,2,10800]{2,1,0:T(2,128)(2,1)S(1)} %reshape.176), channel_id=1, replica_groups=mesh['space'=32,'tm'=8] {'tm'}, dimensions={0} | all-to-all | bytes 691200 | tf_op jit(solution)/shard_map/all_to_all | solution.py:41
  821.5 3.1 reshape.177
  825.7 1.6 fusion.13
  827.6 12.3 %all_to_all.62 = bf16[8,240,90]{2,0,1:T(8,128)(2,1)S(1)} all-to-all(bf16[8,240,90]{2,0,1:T(8,128)(2,1)S(1)} %copy.118), channel_id=1, replica_groups=mesh['space'=32,'tm'=8] {'tm'}, dimensions={1} | all-to-all | bytes 691200 | tf_op jit(solution)/shard_map/all_to_all | solution.py:46
  841.5 2.5 multiply_reduce_fusion.1
  844.0 81.2 %all-reduce = (f32[8]{0:T(128)S(1)}, f32[8]{0:T(128)S(1)}) all-reduce(f32[8]{0:T(128)S(1)} %get-tuple-element.31, f32[8]{0:T(128)S(1)} %get-tuple-element.7), channel_id=1, replica_groups=mesh['space'=32,'tm'=8] {'space','tm'}, use_global_device_ids=true, to_apply=%region_1.2 | all-reduce | flops 16 | bytes 128 | tf_op jit(solution)/shard_map/psum | solution.py:120
  925.2 2.3 multiply_reduce_fusion
  927.5 73.2 %psum.23 = f32[8]{0:T(128)S(1)} all-reduce(f32[8]{0:T(128)S(1)} %get-tuple-element.5), channel_id=1, replica_groups=mesh['space'=32,'tm'=8] {'space','tm'}, use_global_device_ids=true, to_apply=%region_6.7 | all-reduce | flops 8 | bytes 64 | tf_op jit(solution)/shard_map/psum | solution.py:126
  1000.7 2.6 multiply_add_fusion
  (69 shorter events, 31.6 us)
Async XLA Ops:
  7.2 486.0 %copy-start = (bf16[1,8,64,1440]{3,2,1,0:T(8,128)(2,1)S(1)}, bf16[1,8,64,1440]{3,2,1,0:T(8,128)(2,1)}, u32[]{:S(2)}) copy-start(bf16[1,8,64,1440]{3,2,1,0:T(8,128)(2,1)} %param.14) | copy-start | bytes 4423684
  44.4 1.5 copy-start.8
  47.8 9.9 collective-permute-start
  51.2 11.0 %collective-permute-start.1 = (bf16[8,30,720]{2,0,1:T(8,128)(2,1)}, bf16[8,30,720]{2,0,1:T(8,128)(2,1)}, u32[]{:S(2)}, u32[]{:S(2)}) collective-permute-start(bf16[8,30,720]{2,0,1:T(8,128)(2,1)} %multiply_convert_fusion.6), channel_id=1, source_target_pairs={{8,0},{16,8},{24,16},{32,24},{40,32},{48,40},{56,48},{64,56},{72,6... | collective-permute-start | bytes 1036808 | tf_op jit(solution)/shard_map/ppermute | solution.py:30
  63.5 1.1 copy-start.3
  64.6 2.0 copy-start.5
  65.8 0.9 copy-start.2
  67.5 11.8 %collective-permute-start.2 = (bf16[8,30,720]{2,0,1:T(8,128)(2,1)}, bf16[8,30,720]{2,0,1:T(8,128)(2,1)}, u32[]{:S(2)}, u32[]{:S(2)}) collective-permute-start(bf16[8,30,720]{2,0,1:T(8,128)(2,1)} %fusion.47), channel_id=1, source_target_pairs={{0,8},{8,16},{16,24},{24,32},{32,40},{40,48},{48,56},{56,64},{64,7... | collective-permute-start | bytes 1036808 | tf_op jit(solution)/shard_map/ppermute | solution.py:28
  70.6 9.8 collective-permute-start.3
  172.8 15.1 %copy-start.9 = (s32[1,8]{1,0:T(1,128)S(1)}, s32[1,8]{1,0:T(1,128)}, u32[]{:S(2)}) copy-start(s32[1,8]{1,0:T(1,128)} %param.13) | copy-start | bytes 100
  172.8 250.7 %all-to-all-start.2 = ((bf16[32,2,86400]{2,1,0:T(2,128)(2,1)}), bf16[32,2,86400]{2,1,0:T(2,128)(2,1)}, u32[]{:S(2)}, u32[]{:S(2)}) async-start(bf16[32,2,86400]{2,1,0:T(2,128)(2,1)} %reshape.174), calls=%async_computation.2 | async-start | bytes 22118400 | tf_op jit(solution)/shard_map/all_to_all | solution.py:86
  187.8 574.6 %reduce-scatter.2.cloned.1.call-start = ((), (), s32[]{:S(2)}) async-start(), calls=%async_computation.6 | async-start | bytes 12165120 | tf_op jit(solution)/shard_map/reduce_scatter | solution.py:105
  465.7 27.5 %copy-start.10 = (f32[1,1,64]{2,1,0:T(1,128)S(1)}, f32[1,1,64]{2,1,0:T(1,128)}, u32[]{:S(2)}) copy-start(f32[1,1,64]{2,1,0:T(1,128)} %param.15) | copy-start | bytes 772
  771.6 7.1 collective-permute-start.4
  774.6 8.6 collective-permute-start.5
  784.5 1.1 copy-start.4
  785.6 1.1 copy-start.1
  786.8 7.0 collective-permute-start.6
  789.5 8.3 collective-permute-start.7
  839.9 1.5 copy-start.6
  841.5 83.8 %copy-start.7 = (f32[8,30,720]{2,0,1:T(8,128)S(1)}, f32[8,30,720]{2,0,1:T(8,128)}, u32[]{:S(2)}) copy-start(f32[8,30,720]{2,0,1:T(8,128)} %param.9) | copy-start | bytes 2073604
Sparse Core Ops, SparseCore 0:
  518.7 243.6 reduce-scatter.1
